TPU v7x, 32 devices: a whole 2x2x4 slice. The times are simulated.
32 devices in a mesh: sib: 2 (over core), row: 4 (over z), col: 4 (over y, x).
Axes of the slice: x: 2, y: 2, z: 4, core: 2. Of those that a mesh axis runs over, the one named last changes fastest.
Arguments:
- child_front: float32 [2, 2048, 2048], P('sib', 'row', 'col'), may hold values from -6 to 6
- child_panel: float32 [2, 2048, 1024], P('sib', ('row', 'col')), may hold values from -0.42 to 0.42
- block_map: int32 [2, 16], replicated, may hold values from 0 to 23, as said below
- parent_front: float32 [3072, 3072], P(('row', 'sib'), 'col'), may hold values from -6 to 6
- pivot_inverse: float32 [512, 512], replicated, may hold values from -0.03 to 0.1, as said below
Outputs:
- parent_out: float32 [3072, 3072], P(('row', 'sib'), 'col')
Inputs may be any that keep to these rules, and one draw needn't show every extreme that they name: `block_map`: each row is strictly increasing. A child block i that lands in parent block g * 6 + k with 0 <= k < 6 satisfies g * 4 - 2 <= i < (g + 1) * 4; the lower end is met for g = 1 in every draw, and the last parent block is always named. `pivot_inverse`: lower triangular with diagonal entries from 0.05 to 0.1.
All inputs are finite; a program needn't handle non-finite values.
Results may differ from a plain program's by a relative error of at most 0.0001.
Values sent between devices are 32-bit elements; how exact they have to be, the bound alone decides.
No kernel may reach another device: no remote copies, remote signals or barrier semaphores. Data moves between devices by JAX's collectives and lax.ppermute only.
A program may use at most 64 MiB of HBM per device.

v0:
```python
import jax
import jax.numpy as jnp
from jax import lax
from jax.sharding import PartitionSpec as P

BLK = 128
CBD = 4
PBD = 6
HB = 2
PANEL = 512


def from_root(value, axis, source):
    kept = jnp.where(lax.axis_index(axis) == source, value, 0).astype(value.dtype)
    return lax.psum(kept, axis)


def shifted(value, axis, steps):
    count = lax.axis_size(axis)
    initial, last = (max(0, -steps), min(count, count - steps))
    return lax.ppermute(value, axis, [(source, source + steps) for source in range(initial, last)])


def choose_blocks(block_row, device, child_span, parent_span, edge_span):
    padded = jnp.concatenate([jnp.full((edge_span,), -1, jnp.int32), block_row])
    window = lax.dynamic_slice_in_dim(padded, device * child_span, child_span + edge_span)
    target = device * parent_span + jnp.arange(parent_span, dtype=jnp.int32)
    return (window[None, :] == target[:, None]).astype(jnp.float32)


def times_inverse(rows_part, pivot_inverse):
    return lax.dot_general(
        rows_part,
        pivot_inverse,
        (((1,), (1,)), ((), ())),
        precision=lax.Precision.HIGHEST,
        preferred_element_type=jnp.float32,
    )


def shards(child_front, child_panel, block_map, parent_front, pivot_inverse):
    front_index = lax.axis_index("sib")
    row_index = lax.axis_index("row")
    col_index = lax.axis_index("col")
    child_rows = child_front.shape[1]
    parent_rows = parent_front.shape[0]
    parent_cols = parent_front.shape[1]
    edge_width = HB * BLK
    span_blocks = CBD + HB
    rows_local = lax.all_gather(child_panel, "col", axis=1, tiled=True)[0]
    cols_local = from_root(rows_local, "row", col_index)
    update = child_front[0] - lax.dot_general(
        rows_local,
        cols_local,
        (((1,), (1,)), ((), ())),
        precision=lax.Precision.HIGHEST,
        preferred_element_type=jnp.float32,
    )
    my_map = lax.dynamic_index_in_dim(block_map, front_index, 0, keepdims=False)
    left_cols = shifted(update[:, -edge_width:], "col", 1)
    col_window = jnp.concatenate([left_cols, update], axis=1).reshape(child_rows, span_blocks, BLK)
    col_pick = choose_blocks(my_map, col_index, CBD, PBD, HB)
    spread_cols = jnp.einsum(
        "rwk,qw->rqk", col_window, col_pick, precision=lax.Precision.HIGHEST
    ).reshape(child_rows, PBD * BLK)
    left_rows = shifted(spread_cols[-edge_width:], "row", 1)
    row_window = jnp.concatenate([left_rows, spread_cols], axis=0).reshape(
        span_blocks, BLK, PBD * BLK
    )
    row_pick = choose_blocks(my_map, row_index, CBD, PBD, HB)
    spread_both = jnp.einsum(
        "wtc,qw->qtc", row_window, row_pick, precision=lax.Precision.HIGHEST
    ).reshape(PBD * BLK, PBD * BLK)
    summed = lax.psum_scatter(spread_both, "sib", scatter_dimension=0, tiled=True)
    assembled = parent_front + summed
    local_factor = times_inverse(assembled[:, :PANEL], pivot_inverse)
    factor_rows = from_root(local_factor, "col", 0)
    owner_rows = from_root(factor_rows, "row", col_index)
    col_factor = lax.all_gather(owner_rows, "sib", axis=0, tiled=True)
    product = lax.dot_general(
        factor_rows,
        col_factor,
        (((1,), (1,)), ((), ())),
        precision=lax.Precision.HIGHEST,
        preferred_element_type=jnp.float32,
    )
    global_rows = (row_index * 2 + front_index) * parent_rows + jnp.arange(
        parent_rows, dtype=jnp.int32
    )
    global_cols = col_index * parent_cols + jnp.arange(parent_cols, dtype=jnp.int32)
    inside = (global_rows[:, None] >= PANEL) & (global_cols[None, :] >= PANEL)
    trailing = jnp.where(inside, assembled - product, assembled)
    factor_wide = jnp.pad(factor_rows, ((0, 0), (0, parent_cols - PANEL)))
    return jnp.where(global_cols[None, :] < PANEL, factor_wide, trailing)


def solution(mesh):
    in_specs = (
        P("sib", "row", "col"),
        P("sib", ("row", "col"), None),
        P(),
        P(("row", "sib"), "col"),
        P(),
    )
    out_specs = P(("row", "sib"), "col")
    return jax.shard_map(shards, mesh=mesh, in_specs=in_specs, out_specs=out_specs, check_vma=False)
```

profile of v0, /device:TPU:0, one launch (start us, length us, event | category | flops | bytes accessed | tf_op | source)
XLA Modules:
  0.0 330.3 jit_solution(467878976344165727)
XLA Ops:
  6.5 0.0 copy-start
  6.5 0.0 all-gather.3.cloned.1.call-start
  6.5 0.7 all-gather.3.cloned.1.call-update
  7.3 0.0 all-reduce.6.cloned.1.call-start
  7.3 39.8 %all-gather.3.cloned.1.call-done = f32[1,512,1024]{2,1,0:T(8,128)} async-done(((f32[1,128,1024]{2,1,0:T(8,128)}), f32[1,512,1024]{2,1,0:T(8,128)}) %all-gather.3.cloned.1.call-update) | async-done | bytes 2097168 | tf_op jit(solution)/shard_map/all_gather | solution.py:50
  47.1 3.2 bitcast_select_fusion
  50.3 0.0 copy-start.1
  50.3 0.0 all-reduce.6.cloned.1.call-update
  50.4 0.0 reduce-scatter.2.cloned.1.call-start
  50.4 2.7 copy.8
  53.1 0.0 copy-start.5
  53.1 83.6 %all-reduce.6.cloned.1.call-done = f32[512,1024]{1,0:T(8,128)} async-done(((f32[512,1024]{1,0:T(8,128)}), f32[512,1024]{1,0:T(8,128)}) %all-reduce.6.cloned.1.call-update) | async-done | bytes 2097168 | tf_op jit(solution)/shard_map/psum | solution.py:15
  136.7 0.0 copy-done.1
  136.7 5.4 %fusion.8 = f32[512,512]{0,1:T(8,128)S(1)} fusion(f32[512,1024]{1,0:T(8,128)} %all-reduce.6.cloned.1.call-done, f32[1,512,1024]{2,1,0:T(8,128)S(1)} %copy-done.1, f32[1,512,512]{1,2,0:T(8,128)} %copy.8), kind=kOutput, calls=%fused_computation.11 | convolution fusion | flops 3221487616 | bytes 6291456 | tf_op jit(solution)/shard_map/dot_general | solution.py:52
  142.1 0.0 copy-start.2
  142.1 1.0 copy-done.2
  143.1 3.4 %collective-permute-start = (f32[512,256]{0,1:T(8,128)S(1)}, f32[512,256]{0,1:T(8,128)S(1)}, u32[]{:S(2)}, u32[]{:S(2)}) collective-permute-start(f32[512,256]{0,1:T(8,128)S(1)} %slice.16), channel_id=1, source_target_pairs={{0,1},{1,2},{2,3},{4,5},{5,6},{6,7},{8,9},{9,10},{10,11},{12,13},{... | collective-permute-start | bytes 1572872 | tf_op jit(solution)/shard_map/ppermute | solution.py:21
  146.5 0.0 copy-done.5
  146.6 0.1 pad_dynamic-slice_fusion.1
  146.7 10.7 %collective-permute-done = f32[512,256]{0,1:T(8,128)S(1)} collective-permute-done((f32[512,256]{0,1:T(8,128)S(1)}, f32[512,256]{0,1:T(8,128)S(1)}, u32[]{:S(2)}, u32[]{:S(2)}) %collective-permute-start) | collective-permute-done | bytes 524320 | tf_op jit(solution)/shard_map/ppermute | solution.py:21
  157.3 1.3 pad_maximum_fusion.1
  158.7 1.8 copy.9
  160.5 2.7 convolution_bitcast_fusion
  163.2 1.0 slice.17
  164.2 2.4 copy.10
  166.6 3.0 collective-permute-start.1
  169.6 1.7 copy.11
  171.3 13.2 %collective-permute-done.1 = f32[256,768]{0,1:T(8,128)} collective-permute-done((f32[256,768]{0,1:T(8,128)}, f32[256,768]{0,1:T(8,128)}, u32[]{:S(2)}, u32[]{:S(2)}) %collective-permute-start.1) | collective-permute-done | bytes 786464 | tf_op jit(solution)/shard_map/ppermute | solution.py:21
  184.5 3.2 pad_maximum_fusion
  187.7 2.0 copy.12
  189.7 2.9 fusion
  192.6 2.2 copy.14
  194.8 0.0 copy-start.4
  194.8 0.0 reduce-scatter.2.cloned.1.call-update
  194.8 0.2 all-reduce.8.cloned.1.call-start
  195.0 13.4 %reduce-scatter.2.cloned.1.call-done = f32[384,768]{1,0:T(8,128)} async-done(((f32[768,768]{1,0:T(8,128)}), f32[384,768]{1,0:T(8,128)}) %reduce-scatter.2.cloned.1.call-update) | async-done | bytes 1179664 | tf_op jit(solution)/shard_map/reduce_scatter | solution.py:74
  208.4 0.0 copy-done.4
  208.4 1.4 add.80
  209.8 0.0 copy-done
  209.8 2.3 convolution_select_fusion
  212.1 0.0 all-reduce.8.cloned.1.call-update
  212.2 0.0 all-reduce.10.cloned.1.call-start
  212.2 50.0 %all-reduce.8.cloned.1.call-done = f32[384,512]{1,0:T(8,128)} async-done(((f32[384,512]{1,0:T(8,128)}), f32[384,512]{1,0:T(8,128)}) %all-reduce.8.cloned.1.call-update) | async-done | bytes 786448 | tf_op jit(solution)/shard_map/psum | solution.py:15
  262.2 0.0 copy-start.3
  262.2 2.1 broadcast_select_fusion
  264.4 0.0 all-reduce.10.cloned.1.call-update
  264.4 0.0 all-gather.5.cloned.1.call-start
  264.5 44.0 %all-reduce.10.cloned.1.call-done = f32[384,512]{1,0:T(8,128)} async-done(((f32[384,512]{1,0:T(8,128)}), f32[384,512]{1,0:T(8,128)}) %all-reduce.10.cloned.1.call-update) | async-done | bytes 786448 | tf_op jit(solution)/shard_map/psum | solution.py:15
  308.4 0.0 all-gather.5.cloned.1.call-update
  308.5 10.4 %all-gather.5.cloned.1.call-done = f32[768,512]{1,0:T(8,128)} async-done(((f32[384,512]{1,0:T(8,128)}), f32[768,512]{1,0:T(8,128)}) %all-gather.5.cloned.1.call-update) | async-done | bytes 1572880 | tf_op jit(solution)/shard_map/all_gather | solution.py:79
  318.9 0.0 copy-done.3
  318.9 4.6 %fusion.4 = f32[384,768]{1,0:T(8,128)} fusion(f32[384,768]{1,0:T(8,128)S(1)} %add.80, f32[384,512]{1,0:T(8,128)S(1)} %copy-done.3, f32[768,512]{1,0:T(8,128)} %all-gather.5.cloned.1.call-done, pred[768]{0:T(1024)(128)(4,1)S(1)} %get-tuple-element.7, pred[768]{0:T(1024)(128)(4,1)S(1)} %get-tuple-element.8, pred[384]{0:T(512)(128)(4,1)S(1)} %add_compare_fusion), kind=kOutput, calls=%fused_computation.9 | convolution fusion | flops 1813118976 | bytes 4720512 | tf_op jit(solution)/shard_map/dot_general | solution.py:80
  (6 shorter events, 0.1 us)
Async XLA Ops:
  6.5 203.3 %copy-start = (f32[512,512]{1,0:T(8,128)S(1)}, f32[512,512]{1,0:T(8,128)}, u32[]{:S(2)}) copy-start(f32[512,512]{1,0:T(8,128)} %param.9) | copy-start | bytes 3145732
  6.5 40.6 %all-gather.3.cloned.1.call-start = ((), (), s32[]{:S(2)}) async-start(), calls=%async_computation.1 | async-start | bytes 2621440 | tf_op jit(solution)/shard_map/all_gather | solution.py:50
  7.3 129.4 %all-reduce.6.cloned.1.call-start = ((), (), s32[]{:S(2)}) async-start(), calls=%async_computation.2 | async-start | bytes 4194304 | tf_op jit(solution)/shard_map/psum | solution.py:15
  50.3 86.3 %copy-start.1 = (f32[1,512,1024]{2,1,0:T(8,128)S(1)}, f32[1,512,1024]{2,1,0:T(8,128)}, u32[]{:S(2)}) copy-start(f32[1,512,1024]{2,1,0:T(8,128)} %all-gather.3.cloned.1.call-done) | copy-start | bytes 6291460
  50.4 158.0 %reduce-scatter.2.cloned.1.call-start = ((), (), s32[]{:S(2)}) async-start(), calls=%async_computation.3 | async-start | bytes 3538944 | tf_op jit(solution)/shard_map/reduce_scatter | solution.py:74
  53.1 93.4 %copy-start.5 = (s32[2,16]{1,0:T(2,128)S(1)}, s32[2,16]{1,0:T(2,128)}, u32[]{:S(2)}) copy-start(s32[2,16]{1,0:T(2,128)} %param.7) | copy-start | bytes 388
  142.1 1.0 copy-start.2
  143.1 14.2 %collective-permute-start = (f32[512,256]{0,1:T(8,128)S(1)}, f32[512,256]{0,1:T(8,128)S(1)}, u32[]{:S(2)}, u32[]{:S(2)}) collective-permute-start(f32[512,256]{0,1:T(8,128)S(1)} %slice.16), channel_id=1, source_target_pairs={{0,1},{1,2},{2,3},{4,5},{5,6},{6,7},{8,9},{9,10},{10,11},{12,13},{... | collective-permute-start | bytes 1572872 | tf_op jit(solution)/shard_map/ppermute | solution.py:21
  166.6 17.9 %collective-permute-start.1 = (f32[256,768]{0,1:T(8,128)}, f32[256,768]{0,1:T(8,128)}, u32[]{:S(2)}, u32[]{:S(2)}) collective-permute-start(f32[256,768]{0,1:T(8,128)} %bitcast.38), channel_id=1, source_target_pairs={{0,4},{4,8},{8,12},{1,5},{5,9},{9,13},{2,6},{6,10},{10,14},{3,7},{... | collective-permute-start | bytes 2359304 | tf_op jit(solution)/shard_map/ppermute | solution.py:21
  194.8 13.6 %copy-start.4 = (f32[384,768]{1,0:T(8,128)S(1)}, f32[384,768]{1,0:T(8,128)}, u32[]{:S(2)}) copy-start(f32[384,768]{1,0:T(8,128)} %param.8) | copy-start | bytes 3538948
  194.8 67.4 %all-reduce.8.cloned.1.call-start = ((), (), s32[]{:S(2)}) async-start(), calls=%async_computation.4 | async-start | bytes 1572864 | tf_op jit(solution)/shard_map/psum | solution.py:15
  212.2 96.2 %all-reduce.10.cloned.1.call-start = ((), (), s32[]{:S(2)}) async-start(), calls=%async_computation.5 | async-start | bytes 1572864 | tf_op jit(solution)/shard_map/psum | solution.py:15
  262.2 56.7 %copy-start.3 = (f32[384,512]{1,0:T(8,128)S(1)}, f32[384,512]{1,0:T(8,128)}, u32[]{:S(2)}) copy-start(f32[384,512]{1,0:T(8,128)} %all-reduce.8.cloned.1.call-done) | copy-start | bytes 2359300
  264.4 54.5 %all-gather.5.cloned.1.call-start = ((), (), s32[]{:S(2)}) async-start(), calls=%async_computation.6 | async-start | bytes 2359296 | tf_op jit(solution)/shard_map/all_gather | solution.py:79
Sparse Core Ops, SparseCore 0:
  9.2 37.8 all-gather.2
  50.5 86.1 all-reduce.5
  194.9 13.4 reduce-scatter.1
  212.3 49.8 all-reduce.7
  264.5 43.8 all-reduce.9
  309.8 9.0 all-gather.4
where the time goes:
time: 331 us; the launch traced here: 330 us
  waiting for transfers between devices  266 us (80%)
  matrix products  17.9 us (5%)
  local copies, waits for them, and re-layouts  14.9 us (5%)
  between operations  13.6 us (4%)
  other arithmetic  11.4 us (3%)
  starting transfers between devices  6.82 us (2%)
    psum x3, waiting for transfers between devices, from_root(): return lax.psum(kept, axis)  178 us
    all_gather x1, waiting for transfers between devices, shards(): rows_local = lax.all_gather(child_panel, 'col', axis=1, tiled=True)[0]  39.8 us
    ppermute x2, waiting for transfers between devices, shifted(): lax.ppermute(value, axis, [(source, source + steps) for source in range(i...  23.8 us
    reduce_scatter x1, waiting for transfers between devices, shards(): lax.psum_scatter(spread_both, 'sib', scatter_dimension=0, tiled=True)  13.4 us
    all_gather x1, waiting for transfers between devices, shards(): col_factor = lax.all_gather(owner_rows, 'sib', axis=0, tiled=True)  10.4 us
  transfers between devices with their start and end apart: 8, of which 8 were waited for; matrix products, arithmetic and copies ran while one was open for 1% of the time, Pallas kernels for 0%

commit v1 on v0

--- a/solution.py
+++ b/solution.py
@@ -1,3 +1,4 @@
+import functools
 import jax
 import jax.numpy as jnp
 from jax import lax
@@ -8,6 +9,15 @@
 PBD = 6
 HB = 2
 PANEL = 512
+
+
+def units_trace(mine, in_dim, net_axis):
+    val = jnp.stack([mine for _ in range(lax.axis_size(net_axis))])
+    reply = lax.all_to_all(val, net_axis, 0, 0)
+    return jnp.concatenate(reply, in_dim)
+
+
+review_cubes_by_axis = functools.partial(units_trace, in_dim=1, net_axis="col")
 
 
 def from_root(value, axis, source):
@@ -47,7 +57,7 @@
     parent_cols = parent_front.shape[1]
     edge_width = HB * BLK
     span_blocks = CBD + HB
-    rows_local = lax.all_gather(child_panel, "col", axis=1, tiled=True)[0]
+    rows_local = review_cubes_by_axis(child_panel)[0]
     cols_local = from_root(rows_local, "row", col_index)
     update = child_front[0] - lax.dot_general(
         rows_local,

time: 331 us -> 321 us (0.970)
  waiting for transfers between devices: 266 us -> 251 us
  starting transfers between devices: 6.82 us -> 12 us
    all_gather x1 -> x0, waiting for transfers between devices: 39.8 us -> none  [shards(): rows_local = lax.all_gather(child_panel, 'col', axis=1, tiled=True)[0]]
    all_to_all x0 -> x1, waiting for transfers between devices: none -> 24.9 us  [units_trace(): reply = lax.all_to_all(val, net_axis, 0, 0)]
    all_to_all x0 -> x1, starting transfers between devices: none -> 5.19 us  [units_trace(): reply = lax.all_to_all(val, net_axis, 0, 0)]
where the time goes in v1:
time: 321 us
  waiting for transfers between devices  251 us (78%)
  matrix products  17.9 us (6%)
  local copies, waits for them, and re-layouts  17.5 us (5%)
  between operations  13.3 us (4%)
  starting transfers between devices  12 us (4%)
  other arithmetic  9.63 us (3%)
    psum x3, waiting for transfers between devices, from_root(): return lax.psum(kept, axis)  178 us
    all_to_all x1, waiting for transfers between devices, units_trace(): reply = lax.all_to_all(val, net_axis, 0, 0)  24.9 us
    ppermute x2, waiting for transfers between devices, shifted(): lax.ppermute(value, axis, [(source, source + steps) for source in range(i...  23.9 us
    reduce_scatter x1, waiting for transfers between devices, shards(): lax.psum_scatter(spread_both, 'sib', scatter_dimension=0, tiled=True)  13.3 us
    all_gather x1, waiting for transfers between devices, shards(): col_factor = lax.all_gather(owner_rows, 'sib', axis=0, tiled=True)  10.4 us
    ppermute x2, starting transfers between devices, shifted(): lax.ppermute(value, axis, [(source, source + steps) for source in range(i...  6.42 us
  transfers between devices with their start and end apart: 8, of which 8 were waited for; matrix products, arithmetic and copies ran while one was open for 1% of the time, Pallas kernels for 0%

profile of v1, /device:TPU:0, one launch (start us, length us, event | category | flops | bytes accessed | tf_op | source)
XLA Modules:
  0.0 320.9 jit_solution(10532591044226627049)
XLA Ops:
  6.5 0.0 copy-start
  6.5 2.7 stack.2
  9.3 5.2 %all-to-all-start = ((f32[4,1,128,1024]{3,2,1,0:T(8,128)}), f32[4,1,128,1024]{3,2,1,0:T(8,128)S(1)}, u32[]{:S(2)}, u32[]{:S(2)}) async-start(f32[4,1,128,1024]{3,2,1,0:T(8,128)} %stack.2), calls=%async_computation | async-start | bytes 4194304 | tf_op jit(solution)/shard_map/all_to_all | solution.py:16
  14.5 0.0 all-reduce.6.cloned.1.call-start
  14.5 24.9 %all-to-all-done = f32[4,1,128,1024]{3,2,1,0:T(8,128)S(1)} async-done(((f32[4,1,128,1024]{3,2,1,0:T(8,128)}), f32[4,1,128,1024]{3,2,1,0:T(8,128)S(1)}, u32[]{:S(2)}, u32[]{:S(2)}) %all-to-all-start) | async-done | bytes 2097184 | tf_op jit(solution)/shard_map/all_to_all | solution.py:16
  39.3 1.5 broadcast_select_fusion
  40.8 0.0 all-reduce.6.cloned.1.call-update
  40.9 0.0 reduce-scatter.2.cloned.1.call-start
  40.9 2.5 copy.15
  43.4 84.1 %all-reduce.6.cloned.1.call-done = f32[512,1024]{1,0:T(8,128)} async-done(((f32[512,1024]{1,0:T(8,128)}), f32[512,1024]{1,0:T(8,128)}) %all-reduce.6.cloned.1.call-update) | async-done | bytes 2097168 | tf_op jit(solution)/shard_map/psum | solution.py:25
  127.6 0.0 copy-start.4
  127.6 5.4 %fusion.3 = f32[512,512]{0,1:T(8,128)S(1)} fusion(f32[512,1024]{1,0:T(8,128)} %all-reduce.6.cloned.1.call-done, f32[512,1024]{1,0:T(8,128)S(1)} %bitcast.30, f32[1,512,512]{1,2,0:T(8,128)} %copy.15), kind=kOutput, calls=%fused_computation.8 | convolution fusion | flops 3221487616 | bytes 6291456 | tf_op jit(solution)/shard_map/dot_general | solution.py:62
  133.0 0.0 copy-start.1
  133.0 1.0 copy-done.1
  134.0 3.4 %collective-permute-start = (f32[512,256]{0,1:T(8,128)S(1)}, f32[512,256]{0,1:T(8,128)S(1)}, u32[]{:S(2)}, u32[]{:S(2)}) collective-permute-start(f32[512,256]{0,1:T(8,128)S(1)} %slice.16), channel_id=1, source_target_pairs={{0,1},{1,2},{2,3},{4,5},{5,6},{6,7},{8,9},{9,10},{10,11},{12,13},{... | collective-permute-start | bytes 1572872 | tf_op jit(solution)/shard_map/ppermute | solution.py:31
  137.4 0.0 copy-done.4
  137.5 0.1 pad_dynamic-slice_fusion.1
  137.6 10.7 %collective-permute-done = f32[512,256]{0,1:T(8,128)S(1)} collective-permute-done((f32[512,256]{0,1:T(8,128)S(1)}, f32[512,256]{0,1:T(8,128)S(1)}, u32[]{:S(2)}, u32[]{:S(2)}) %collective-permute-start) | collective-permute-done | bytes 524320 | tf_op jit(solution)/shard_map/ppermute | solution.py:31
  148.2 1.3 pad_maximum_fusion.1
  149.6 1.8 copy.16
  151.4 2.7 convolution_bitcast_fusion
  154.1 1.0 slice.17
  155.1 2.4 copy.17
  157.5 3.0 collective-permute-start.1
  160.5 1.6 copy.18
  162.2 13.2 %collective-permute-done.1 = f32[256,768]{0,1:T(8,128)} collective-permute-done((f32[256,768]{0,1:T(8,128)}, f32[256,768]{0,1:T(8,128)}, u32[]{:S(2)}, u32[]{:S(2)}) %collective-permute-start.1) | collective-permute-done | bytes 786464 | tf_op jit(solution)/shard_map/ppermute | solution.py:31
  175.4 3.2 pad_maximum_fusion
  178.6 2.0 copy.19
  180.6 2.9 fusion
  183.5 2.2 copy.21
  185.7 0.0 copy-start.3
  185.7 0.0 reduce-scatter.2.cloned.1.call-update
  185.7 0.2 all-reduce.8.cloned.1.call-start
  185.9 13.3 %reduce-scatter.2.cloned.1.call-done = f32[384,768]{1,0:T(8,128)} async-done(((f32[768,768]{1,0:T(8,128)}), f32[384,768]{1,0:T(8,128)}) %reduce-scatter.2.cloned.1.call-update) | async-done | bytes 1179664 | tf_op jit(solution)/shard_map/reduce_scatter | solution.py:84
  199.3 0.0 copy-done.3
  199.3 1.4 add.80
  200.7 0.0 copy-done
  200.7 2.3 convolution_select_fusion
  203.0 0.0 all-reduce.8.cloned.1.call-update
  203.1 0.0 all-reduce.10.cloned.1.call-start
  203.1 50.0 %all-reduce.8.cloned.1.call-done = f32[384,512]{1,0:T(8,128)} async-done(((f32[384,512]{1,0:T(8,128)}), f32[384,512]{1,0:T(8,128)}) %all-reduce.8.cloned.1.call-update) | async-done | bytes 786448 | tf_op jit(solution)/shard_map/psum | solution.py:25
  253.1 0.0 copy-start.2
  253.1 2.1 broadcast_select_fusion.1
  255.3 0.0 all-reduce.10.cloned.1.call-update
  255.3 0.0 all-gather.2.cloned.1.call-start
  255.4 44.0 %all-reduce.10.cloned.1.call-done = f32[384,512]{1,0:T(8,128)} async-done(((f32[384,512]{1,0:T(8,128)}), f32[384,512]{1,0:T(8,128)}) %all-reduce.10.cloned.1.call-update) | async-done | bytes 786448 | tf_op jit(solution)/shard_map/psum | solution.py:25
  299.3 0.0 all-gather.2.cloned.1.call-update
  299.4 10.4 %all-gather.2.cloned.1.call-done = f32[768,512]{1,0:T(8,128)} async-done(((f32[384,512]{1,0:T(8,128)}), f32[768,512]{1,0:T(8,128)}) %all-gather.2.cloned.1.call-update) | async-done | bytes 1572880 | tf_op jit(solution)/shard_map/all_gather | solution.py:89
  309.8 0.0 copy-done.2
  309.8 4.6 %fusion.2 = f32[384,768]{1,0:T(8,128)} fusion(f32[384,768]{1,0:T(8,128)S(1)} %add.80, f32[384,512]{1,0:T(8,128)S(1)} %copy-done.2, f32[768,512]{1,0:T(8,128)} %all-gather.2.cloned.1.call-done, pred[768]{0:T(1024)(128)(4,1)S(1)} %get-tuple-element.7, pred[768]{0:T(1024)(128)(4,1)S(1)} %get-tuple-element.8, pred[384]{0:T(512)(128)(4,1)S(1)} %add_compare_fusion), kind=kOutput, calls=%fused_computation.6 | convolution fusion | flops 1813118976 | bytes 4720512 | tf_op jit(solution)/shard_map/dot_general | solution.py:90
  (6 shorter events, 0.1 us)
Async XLA Ops:
  6.5 194.2 %copy-start = (f32[512,512]{1,0:T(8,128)S(1)}, f32[512,512]{1,0:T(8,128)}, u32[]{:S(2)}) copy-start(f32[512,512]{1,0:T(8,128)} %param.9) | copy-start | bytes 3145732
  9.3 30.1 %all-to-all-start = ((f32[4,1,128,1024]{3,2,1,0:T(8,128)}), f32[4,1,128,1024]{3,2,1,0:T(8,128)S(1)}, u32[]{:S(2)}, u32[]{:S(2)}) async-start(f32[4,1,128,1024]{3,2,1,0:T(8,128)} %stack.2), calls=%async_computation | async-start | bytes 4194304 | tf_op jit(solution)/shard_map/all_to_all | solution.py:16
  14.5 113.1 %all-reduce.6.cloned.1.call-start = ((), (), s32[]{:S(2)}) async-start(), calls=%async_computation.2 | async-start | bytes 4194304 | tf_op jit(solution)/shard_map/psum | solution.py:25
  40.9 158.4 %reduce-scatter.2.cloned.1.call-start = ((), (), s32[]{:S(2)}) async-start(), calls=%async_computation.3 | async-start | bytes 3538944 | tf_op jit(solution)/shard_map/reduce_scatter | solution.py:84
  127.6 9.9 %copy-start.4 = (s32[2,16]{1,0:T(2,128)S(1)}, s32[2,16]{1,0:T(2,128)}, u32[]{:S(2)}) copy-start(s32[2,16]{1,0:T(2,128)} %param.7) | copy-start | bytes 388
  133.0 1.0 copy-start.1
  134.0 14.2 %collective-permute-start = (f32[512,256]{0,1:T(8,128)S(1)}, f32[512,256]{0,1:T(8,128)S(1)}, u32[]{:S(2)}, u32[]{:S(2)}) collective-permute-start(f32[512,256]{0,1:T(8,128)S(1)} %slice.16), channel_id=1, source_target_pairs={{0,1},{1,2},{2,3},{4,5},{5,6},{6,7},{8,9},{9,10},{10,11},{12,13},{... | collective-permute-start | bytes 1572872 | tf_op jit(solution)/shard_map/ppermute | solution.py:31
  157.5 17.9 %collective-permute-start.1 = (f32[256,768]{0,1:T(8,128)}, f32[256,768]{0,1:T(8,128)}, u32[]{:S(2)}, u32[]{:S(2)}) collective-permute-start(f32[256,768]{0,1:T(8,128)} %bitcast.35), channel_id=1, source_target_pairs={{0,4},{4,8},{8,12},{1,5},{5,9},{9,13},{2,6},{6,10},{10,14},{3,7},{... | collective-permute-start | bytes 2359304 | tf_op jit(solution)/shard_map/ppermute | solution.py:31
  185.7 13.6 %copy-start.3 = (f32[384,768]{1,0:T(8,128)S(1)}, f32[384,768]{1,0:T(8,128)}, u32[]{:S(2)}) copy-start(f32[384,768]{1,0:T(8,128)} %param.8) | copy-start | bytes 3538948
  185.7 67.4 %all-reduce.8.cloned.1.call-start = ((), (), s32[]{:S(2)}) async-start(), calls=%async_computation.4 | async-start | bytes 1572864 | tf_op jit(solution)/shard_map/psum | solution.py:25
  203.1 96.3 %all-reduce.10.cloned.1.call-start = ((), (), s32[]{:S(2)}) async-start(), calls=%async_computation.5 | async-start | bytes 1572864 | tf_op jit(solution)/shard_map/psum | solution.py:25
  253.1 56.6 %copy-start.2 = (f32[384,512]{1,0:T(8,128)S(1)}, f32[384,512]{1,0:T(8,128)}, u32[]{:S(2)}) copy-start(f32[384,512]{1,0:T(8,128)} %all-reduce.8.cloned.1.call-done) | copy-start | bytes 2359300
  255.3 54.5 %all-gather.2.cloned.1.call-start = ((), (), s32[]{:S(2)}) async-start(), calls=%async_computation.6 | async-start | bytes 2359296 | tf_op jit(solution)/shard_map/all_gather | solution.py:89
Sparse Core Ops, SparseCore 0:
  41.0 86.5 all-reduce.5
  185.8 13.3 reduce-scatter.1
  203.2 49.9 all-reduce.7
  255.4 43.8 all-reduce.9
  300.7 9.0 all-gather.1
